TPU v7x, 32 devices: a whole 2x2x4 slice. The times are simulated.
32 devices in a mesh: dp: 4 (over y, x), tensor: 8 (over z, core).
Axes of the slice: x: 2, y: 2, z: 4, core: 2. Of those that a mesh axis runs over, the one named last changes fastest.
Arguments:
- latents: bfloat16 [4, 2048, 1152], P('dp', 'tensor'), may hold values from -6 to 6
- conditioning: bfloat16 [4, 1152], P('dp', 'tensor'), may hold values from -6 to 6
- ada_weight: bfloat16 [2, 1152, 6912], P(None, 'tensor'), may hold values from -0.1875 to 0.1875
- ada_bias: bfloat16 [2, 6912], replicated, may hold values from -3 to 3
- qkv_weight: bfloat16 [2, 1152, 3, 1152], P(None, None, None, 'tensor'), may hold values from -0.1875 to 0.1875
- qkv_bias: bfloat16 [2, 2, 1152], P(None, None, 'tensor'), may hold values from -3 to 3
- out_weight: bfloat16 [2, 1152, 1152], P(None, 'tensor'), may hold values from -0.75 to 0.75
- out_bias: bfloat16 [2, 1152], replicated, may hold values from -3 to 3
- fc1_weight: bfloat16 [2, 1152, 4608], P(None, None, 'tensor'), may hold values from -0.1875 to 0.1875
- fc1_bias: bfloat16 [2, 4608], P(None, 'tensor'), may hold values from -3 to 3
- fc2_weight: bfloat16 [2, 4608, 1152], P(None, 'tensor'), may hold values from -0.09375 to 0.09375
- fc2_bias: bfloat16 [2, 1152], replicated, may hold values from -3 to 3
- out_grad: bfloat16 [4, 2048, 1152], P('dp', 'tensor'), may hold values from -6 to 6
Outputs:
- layer_output: bfloat16 [4, 2048, 1152], P('dp', 'tensor')
- latents_grad: bfloat16 [4, 2048, 1152], P('dp', 'tensor')
- conditioning_grad: bfloat16 [4, 1152], P('dp', 'tensor')
- ada_weight_grad: float32 [2, 1152, 6912], P(None, 'tensor')
- ada_bias_grad: float32 [2, 6912], replicated
- qkv_weight_grad: float32 [2, 1152, 3, 1152], P(None, None, None, 'tensor')
- qkv_bias_grad: float32 [2, 2, 1152], P(None, None, 'tensor')
- out_weight_grad: float32 [2, 1152, 1152], P(None, 'tensor')
- out_bias_grad: float32 [2, 1152], replicated
- fc1_weight_grad: float32 [2, 1152, 4608], P(None, None, 'tensor')
- fc1_bias_grad: float32 [2, 4608], P(None, 'tensor')
- fc2_weight_grad: float32 [2, 4608, 1152], P(None, 'tensor')
- fc2_bias_grad: float32 [2, 1152], replicated
All inputs are finite; a program needn't handle non-finite values.
Results may differ from a plain program's by a relative error of at most 0.04.
Values may be sent and summed in bfloat16 or wider, within the bound.
A program may use at most 256 MiB of HBM per device.

v0:
```python
from functools import partial
import jax
import jax.numpy as jnp
from jax import lax
from jax.sharding import PartitionSpec as P

HEAD_DIM = 72
PATCHES = 256
FRAMES = 8
LAYERS = 2


def normalize(stream):
    centered = stream - jnp.mean(stream, axis=-1, keepdims=True)
    variance = jnp.mean(centered * centered, axis=-1, keepdims=True)
    return centered * lax.rsqrt(variance + 1e-06)


def modulate(stream, shift_in, scale_in):
    return normalize(stream) * (1.0 + scale_in) + shift_in


def grouped(token_rows, spatial):
    heads_here = token_rows.shape[1] // HEAD_DIM
    shaped = token_rows.reshape(FRAMES, PATCHES, heads_here, HEAD_DIM)
    if spatial:
        return shaped
    return jnp.transpose(shaped, (1, 0, 2, 3))


def ungrouped(groups, spatial):
    if not spatial:
        groups = jnp.transpose(groups, (1, 0, 2, 3))
    return groups.reshape(FRAMES * PATCHES, groups.shape[2] * HEAD_DIM)


def softmax_rows(query_g, key_g):
    scores = jnp.einsum(
        "gqhd,gkhd->ghqk", query_g, key_g, preferred_element_type=jnp.float32
    ) * HEAD_DIM ** (-0.5)
    return jax.nn.softmax(scores, axis=-1)


def attend(query_rows, key_rows, value_rows, spatial):
    attn_probs = softmax_rows(grouped(query_rows, spatial), grouped(key_rows, spatial)).astype(
        jnp.bfloat16
    )
    mixed = jnp.einsum(
        "ghqk,gkhd->gqhd",
        attn_probs,
        grouped(value_rows, spatial),
        preferred_element_type=jnp.float32,
    )
    return ungrouped(mixed, spatial)


def attend_back(query_rows, key_rows, value_rows, mixed_grad, spatial):
    query_g = grouped(query_rows, spatial)
    key_g = grouped(key_rows, spatial)
    value_g = grouped(value_rows, spatial)
    grad_g = grouped(mixed_grad, spatial)
    probs_full = softmax_rows(query_g, key_g)
    value_grad = jnp.einsum(
        "ghqk,gqhd->gkhd",
        probs_full.astype(jnp.bfloat16),
        grad_g,
        preferred_element_type=jnp.float32,
    )
    probs_grad = jnp.einsum("gqhd,gkhd->ghqk", grad_g, value_g, preferred_element_type=jnp.float32)
    score_grad = probs_full * (
        probs_grad - jnp.sum(probs_grad * probs_full, axis=-1, keepdims=True)
    )
    score_low = score_grad.astype(jnp.bfloat16)
    factor = HEAD_DIM ** (-0.5)
    query_grad = (
        jnp.einsum("ghqk,gkhd->gqhd", score_low, key_g, preferred_element_type=jnp.float32) * factor
    )
    key_grad = (
        jnp.einsum("ghqk,gqhd->gkhd", score_low, query_g, preferred_element_type=jnp.float32)
        * factor
    )
    return (
        ungrouped(query_grad, spatial),
        ungrouped(key_grad, spatial),
        ungrouped(value_grad, spatial),
    )


def spread_rows(row_block):
    return lax.all_gather(row_block, "tensor", axis=0, tiled=True)


def reduce_rows(partial_terms):
    return lax.psum_scatter(
        partial_terms.astype(jnp.bfloat16), "tensor", scatter_dimension=0, tiled=True
    ).astype(jnp.float32)


def spread_grads(row_block):
    return lax.all_gather(row_block, "tensor", axis=0, tiled=True)


def reduce_grads(partial_terms):
    return lax.psum_scatter(
        partial_terms.astype(jnp.bfloat16), "tensor", scatter_dimension=0, tiled=True
    ).astype(jnp.float32)


def layer_forward(stream, modulation, params, spatial):
    qkv_w, qkv_b, out_w, out_b, fc1_w, fc1_b, fc2_w, fc2_b = params
    shift_att, scale_att, gate_att, shift_mlp, scale_mlp, gate_mlp = jnp.split(modulation, 6)
    normed = spread_rows(modulate(stream, shift_att, scale_att).astype(jnp.bfloat16))
    head_width = qkv_w.shape[2]
    projected = jnp.dot(
        normed, qkv_w.reshape(qkv_w.shape[0], 3 * head_width), preferred_element_type=jnp.float32
    )
    query_rows = (projected[:, :head_width] + qkv_b[0].astype(jnp.float32)).astype(jnp.bfloat16)
    key_rows = projected[:, head_width : 2 * head_width].astype(jnp.bfloat16)
    value_rows = (projected[:, 2 * head_width :] + qkv_b[1].astype(jnp.float32)).astype(
        jnp.bfloat16
    )
    heads_out = attend(query_rows, key_rows, value_rows, spatial).astype(jnp.bfloat16)
    attn_branch = reduce_rows(
        jnp.dot(heads_out, out_w, preferred_element_type=jnp.float32)
    ) + out_b.astype(jnp.float32)
    middle = stream + gate_att * attn_branch
    normed_mlp = spread_rows(modulate(middle, shift_mlp, scale_mlp).astype(jnp.bfloat16))
    hidden = jnp.dot(normed_mlp, fc1_w, preferred_element_type=jnp.float32) + fc1_b.astype(
        jnp.float32
    )
    activated = jax.nn.gelu(hidden, approximate=True).astype(jnp.bfloat16)
    mlp_branch = reduce_rows(
        jnp.dot(activated, fc2_w, preferred_element_type=jnp.float32)
    ) + fc2_b.astype(jnp.float32)
    result = middle + gate_mlp * mlp_branch
    saved = (
        normed,
        query_rows,
        key_rows,
        value_rows,
        heads_out,
        attn_branch,
        middle,
        normed_mlp,
        hidden,
        mlp_branch,
    )
    return (result, saved)


def layer_backward(stream, modulation, params, saved, stream_grad, spatial):
    qkv_w, qkv_b, out_w, out_b, fc1_w, fc1_b, fc2_w, fc2_b = params
    (
        normed,
        query_rows,
        key_rows,
        value_rows,
        heads_out,
        attn_branch,
        middle,
        normed_mlp,
        hidden,
        mlp_branch,
    ) = saved
    shift_att, scale_att, gate_att, shift_mlp, scale_mlp, gate_mlp = jnp.split(modulation, 6)
    head_width = qkv_w.shape[2]
    mlp_grad = (gate_mlp * stream_grad).astype(jnp.bfloat16)
    gate_mlp_grad = jnp.sum(stream_grad * mlp_branch, axis=0)
    fc2_b_grad = jnp.sum(mlp_grad, axis=0, dtype=jnp.float32)
    mlp_grad_all = spread_grads(mlp_grad)
    gelu_out, gelu_back = jax.vjp(partial(jax.nn.gelu, approximate=True), hidden)
    activated = gelu_out.astype(jnp.bfloat16)
    fc2_w_grad = jnp.einsum(
        "tf,td->fd", activated, mlp_grad_all, preferred_element_type=jnp.float32
    )
    act_grad = jnp.einsum("td,fd->tf", mlp_grad_all, fc2_w, preferred_element_type=jnp.float32)
    hidden_grad = gelu_back(act_grad)[0].astype(jnp.bfloat16)
    fc1_b_grad = jnp.sum(hidden_grad, axis=0, dtype=jnp.float32)
    fc1_w_grad = jnp.einsum(
        "td,tf->df", normed_mlp, hidden_grad, preferred_element_type=jnp.float32
    )
    mlp_in_grad = reduce_grads(
        jnp.einsum("tf,df->td", hidden_grad, fc1_w, preferred_element_type=jnp.float32)
    )
    _, mlp_norm_back = jax.vjp(modulate, middle, shift_mlp, scale_mlp)
    middle_part, shift_mlp_grad, scale_mlp_grad = mlp_norm_back(mlp_in_grad)
    middle_grad = stream_grad + middle_part
    attn_grad = (gate_att * middle_grad).astype(jnp.bfloat16)
    gate_att_grad = jnp.sum(middle_grad * attn_branch, axis=0)
    out_b_grad = jnp.sum(attn_grad, axis=0, dtype=jnp.float32)
    attn_grad_all = spread_grads(attn_grad)
    out_w_grad = jnp.einsum(
        "tw,td->wd", heads_out, attn_grad_all, preferred_element_type=jnp.float32
    )
    heads_grad = jnp.einsum(
        "td,wd->tw", attn_grad_all, out_w, preferred_element_type=jnp.float32
    ).astype(jnp.bfloat16)
    query_grad, key_grad, value_grad = attend_back(
        query_rows, key_rows, value_rows, heads_grad, spatial
    )
    qkv_grad = jnp.concatenate([query_grad, key_grad, value_grad], axis=1).astype(jnp.bfloat16)
    qkv_b_grad = jnp.stack(
        [
            jnp.sum(qkv_grad[:, :head_width], axis=0, dtype=jnp.float32),
            jnp.sum(qkv_grad[:, 2 * head_width :], axis=0, dtype=jnp.float32),
        ]
    )
    qkv_flat = qkv_w.reshape(qkv_w.shape[0], 3 * head_width)
    qkv_w_grad = jnp.einsum(
        "td,tw->dw", normed, qkv_grad, preferred_element_type=jnp.float32
    ).reshape(qkv_w.shape)
    attn_in_grad = reduce_grads(
        jnp.einsum("tw,dw->td", qkv_grad, qkv_flat, preferred_element_type=jnp.float32)
    )
    _, att_norm_back = jax.vjp(modulate, stream, shift_att, scale_att)
    stream_part, shift_att_grad, scale_att_grad = att_norm_back(attn_in_grad)
    input_grad = middle_grad + stream_part
    modulation_grad = jnp.concatenate(
        [
            shift_att_grad,
            scale_att_grad,
            gate_att_grad,
            shift_mlp_grad,
            scale_mlp_grad,
            gate_mlp_grad,
        ]
    )
    return (
        input_grad,
        modulation_grad,
        (
            qkv_w_grad,
            qkv_b_grad,
            out_w_grad,
            out_b_grad,
            fc1_w_grad,
            fc1_b_grad,
            fc2_w_grad,
            fc2_b_grad,
        ),
    )


def per_device(
    latents,
    conditioning,
    ada_weight,
    ada_bias,
    qkv_weight,
    qkv_bias,
    out_weight,
    out_bias,
    fc1_weight,
    fc1_bias,
    fc2_weight,
    fc2_bias,
    out_grad,
):
    cond_row = conditioning[0].astype(jnp.float32)
    silu_out, silu_back = jax.vjp(jax.nn.silu, cond_row)
    silu_cond = silu_out.astype(jnp.bfloat16)
    ada_terms = jnp.einsum("d,ldm->lm", silu_cond, ada_weight, preferred_element_type=jnp.float32)
    modulations = lax.psum(ada_terms, "tensor") + ada_bias.astype(jnp.float32)
    stacked = (
        qkv_weight,
        qkv_bias,
        out_weight,
        out_bias,
        fc1_weight,
        fc1_bias,
        fc2_weight,
        fc2_bias,
    )
    stream = latents[0].astype(jnp.float32)
    inputs_kept = []
    saved_all = []
    for layer_idx in range(LAYERS):
        params = tuple((member[layer_idx] for member in stacked))
        inputs_kept.append(stream)
        stream, saved = layer_forward(stream, modulations[layer_idx], params, layer_idx % 2 == 0)
        saved_all.append(saved)
    layer_output = stream.astype(jnp.bfloat16)[None]
    stream_grad = out_grad[0].astype(jnp.float32)
    mod_grads = [None] * LAYERS
    layer_grads = [None] * LAYERS
    for layer_idx in reversed(range(LAYERS)):
        params = tuple((member[layer_idx] for member in stacked))
        spatial = layer_idx % 2 == 0
        saved = layer_forward(inputs_kept[layer_idx], modulations[layer_idx], params, spatial)[1]
        stream_grad, mod_grads[layer_idx], layer_grads[layer_idx] = layer_backward(
            inputs_kept[layer_idx], modulations[layer_idx], params, saved, stream_grad, spatial
        )

    def collect(position):
        return jnp.stack([member[position] for member in layer_grads])

    mod_sum, out_b_sum, fc2_b_sum = (
        lax.psum(jnp.stack(mod_grads).astype(jnp.bfloat16), "tensor").astype(jnp.float32),
        lax.psum(collect(3).astype(jnp.bfloat16), "tensor").astype(jnp.float32),
        lax.psum(collect(7).astype(jnp.bfloat16), "tensor").astype(jnp.float32),
    )
    mod_low = mod_sum.astype(jnp.bfloat16)
    ada_w_grad = (
        silu_cond.astype(jnp.float32)[None, :, None] * mod_low.astype(jnp.float32)[:, None, :]
    )
    ada_b_grad = mod_low.astype(jnp.float32)
    silu_grad = jnp.einsum("lm,ldm->d", mod_low, ada_weight, preferred_element_type=jnp.float32)
    cond_grad = silu_back(silu_grad)[0]
    summed = (
        lax.psum(ada_w_grad.astype(jnp.bfloat16), "dp").astype(jnp.float32),
        lax.psum(ada_b_grad.astype(jnp.bfloat16), "dp").astype(jnp.float32),
        lax.psum(collect(0).astype(jnp.bfloat16), "dp").astype(jnp.float32),
        lax.psum(collect(1).astype(jnp.bfloat16), "dp").astype(jnp.float32),
        lax.psum(collect(2).astype(jnp.bfloat16), "dp").astype(jnp.float32),
        lax.psum(out_b_sum.astype(jnp.bfloat16), "dp").astype(jnp.float32),
        lax.psum(collect(4).astype(jnp.bfloat16), "dp").astype(jnp.float32),
        lax.psum(collect(5).astype(jnp.bfloat16), "dp").astype(jnp.float32),
        lax.psum(collect(6).astype(jnp.bfloat16), "dp").astype(jnp.float32),
        lax.psum(fc2_b_sum.astype(jnp.bfloat16), "dp").astype(jnp.float32),
    )
    return (
        layer_output,
        stream_grad.astype(jnp.bfloat16)[None],
        cond_grad.astype(jnp.bfloat16)[None],
        summed[0],
        summed[1],
        summed[2],
        summed[3],
        summed[4],
        summed[5],
        summed[6],
        summed[7],
        summed[8],
        summed[9],
    )


def solution(mesh):
    in_specs = (
        P("dp", "tensor", None),
        P("dp", "tensor"),
        P(None, "tensor", None),
        P(),
        P(None, None, None, "tensor"),
        P(None, None, "tensor"),
        P(None, "tensor", None),
        P(),
        P(None, None, "tensor"),
        P(None, "tensor"),
        P(None, "tensor", None),
        P(),
        P("dp", "tensor", None),
    )
    out_specs = (
        P("dp", "tensor", None),
        P("dp", "tensor", None),
        P("dp", "tensor"),
        P(None, "tensor", None),
        P(),
        P(None, None, None, "tensor"),
        P(None, None, "tensor"),
        P(None, "tensor", None),
        P(),
        P(None, None, "tensor"),
        P(None, "tensor"),
        P(None, "tensor", None),
        P(),
    )
    return jax.shard_map(
        per_device, mesh=mesh, in_specs=in_specs, out_specs=out_specs, check_vma=False
    )
```

profile of v0, /device:TPU:0, one launch (start us, length us, event | category | flops | bytes accessed | tf_op | source)
XLA Modules:
  0.0 1360.1 jit_solution(16830422912774858308)
XLA Ops:
  14.0 30.9 %psum.98 = f32[2,6912]{1,0:T(2,128)S(1)} all-reduce(f32[2,6912]{1,0:T(2,128)S(1)} %bitcast.362), channel_id=1, replica_groups=mesh['dp'=4,'tensor'=8] {'tensor'}, use_global_device_ids=true, to_apply=%region_0.1 | all-reduce | flops 13824 | bytes 110592 | tf_op jit(solution)/shard_map/psum | solution.py:263
  48.3 48.6 %all-gather.9.cloned.1.call-done = bf16[2048,1152]{1,0:T(8,128)(2,1)} async-done(((bf16[256,1152]{1,0:T(8,128)(2,1)}), bf16[2048,1152]{1,0:T(8,128)(2,1)}) %all-gather.9.cloned.1.call-update) | async-done | bytes 4718608 | tf_op jit(solution)/shard_map/all_gather | solution.py:90
  96.8 5.1 fusion.181
  104.4 3.2 fusion.168
  110.7 3.8 convolution_convert_fusion.7
  115.8 52.6 %reduce-scatter.9.cloned.1.call-done = bf16[256,1152]{1,0:T(8,128)(2,1)} async-done(((bf16[2048,1152]{1,0:T(8,128)(2,1)}), bf16[256,1152]{1,0:T(8,128)(2,1)}) %reduce-scatter.9.cloned.1.call-update) | async-done | bytes 589840 | tf_op jit(solution)/shard_map/reduce_scatter | solution.py:94
  173.6 49.3 %all-gather.11.cloned.1.call-done = bf16[2048,1152]{1,0:T(8,128)(2,1)} async-done(((bf16[256,1152]{1,0:T(8,128)(2,1)}), bf16[2048,1152]{1,0:T(8,128)(2,1)}) %all-gather.11.cloned.1.call-update) | async-done | bytes 4718608 | tf_op jit(solution)/shard_map/all_gather | solution.py:90
  223.0 5.6 fusion.59
  230.9 6.7 convolution_convert_fusion.6
  238.9 52.6 %reduce-scatter.11.cloned.1.call-done = bf16[256,1152]{1,0:T(8,128)(2,1)} async-done(((bf16[2048,1152]{1,0:T(8,128)(2,1)}), bf16[256,1152]{1,0:T(8,128)(2,1)}) %reduce-scatter.11.cloned.1.call-update) | async-done | bytes 589840 | tf_op jit(solution)/shard_map/reduce_scatter | solution.py:94
  294.5 50.2 %all-gather.13.cloned.1.call-done = bf16[2048,1152]{1,0:T(8,128)(2,1)} async-done(((bf16[256,1152]{1,0:T(8,128)(2,1)}), bf16[2048,1152]{1,0:T(8,128)(2,1)}) %all-gather.13.cloned.1.call-update) | async-done | bytes 4718608 | tf_op jit(solution)/shard_map/all_gather | solution.py:90
  344.7 4.8 fusion.182
  356.7 5.3 fusion.169
  362.0 3.7 fusion.40
  368.6 4.8 convolution_convert_fusion.5
  373.4 53.9 %reduce-scatter.13.cloned.1.call-done = bf16[256,1152]{1,0:T(8,128)(2,1)} async-done(((bf16[2048,1152]{1,0:T(8,128)(2,1)}), bf16[256,1152]{1,0:T(8,128)(2,1)}) %reduce-scatter.13.cloned.1.call-update) | async-done | bytes 589840 | tf_op jit(solution)/shard_map/reduce_scatter | solution.py:94
  435.0 47.1 %all-gather.15.cloned.1.call-done = bf16[2048,1152]{1,0:T(8,128)(2,1)} async-done(((bf16[256,1152]{1,0:T(8,128)(2,1)}), bf16[2048,1152]{1,0:T(8,128)(2,1)}) %all-gather.15.cloned.1.call-update) | async-done | bytes 4718608 | tf_op jit(solution)/shard_map/all_gather | solution.py:90
  482.1 8.2 fusion.51
  490.2 44.6 %all-gather.17.cloned.1.call-done = bf16[2048,1152]{1,0:T(8,128)(2,1)} async-done(((bf16[256,1152]{1,0:T(8,128)(2,1)}), bf16[2048,1152]{1,0:T(8,128)(2,1)}) %all-gather.17.cloned.1.call-update) | async-done | bytes 4718608 | tf_op jit(solution)/shard_map/all_gather | solution.py:100
  534.8 9.9 fusion.178
  546.2 5.8 convolution_convert_fusion.3
  552.2 10.0 convolution_convert_fusion.4
  562.3 43.6 %reduce-scatter.17.cloned.1.call-done = bf16[256,1152]{1,0:T(8,128)(2,1)} async-done(((bf16[2048,1152]{1,0:T(8,128)(2,1)}), bf16[256,1152]{1,0:T(8,128)(2,1)}) %reduce-scatter.17.cloned.1.call-update) | async-done | bytes 589840 | tf_op jit(solution)/shard_map/reduce_scatter | solution.py:104
  609.3 52.7 %reduce-scatter.15.cloned.1.call-done = bf16[256,1152]{1,0:T(8,128)(2,1)} async-done(((bf16[2048,1152]{1,0:T(8,128)(2,1)}), bf16[256,1152]{1,0:T(8,128)(2,1)}) %reduce-scatter.15.cloned.1.call-update) | async-done | bytes 589840 | tf_op jit(solution)/shard_map/reduce_scatter | solution.py:94
  667.7 50.0 %all-gather.19.cloned.1.call-done = bf16[2048,1152]{1,0:T(8,128)(2,1)} async-done(((bf16[256,1152]{1,0:T(8,128)(2,1)}), bf16[2048,1152]{1,0:T(8,128)(2,1)}) %all-gather.19.cloned.1.call-update) | async-done | bytes 4718608 | tf_op jit(solution)/shard_map/all_gather | solution.py:100
  717.7 4.0 convolution_convert_fusion.17
  723.7 4.3 fusion.174
  744.6 4.6 convolution_convert_fusion.1
  749.3 53.9 %reduce-scatter.19.cloned.1.call-done = bf16[256,1152]{1,0:T(8,128)(2,1)} async-done(((bf16[2048,1152]{1,0:T(8,128)(2,1)}), bf16[256,1152]{1,0:T(8,128)(2,1)}) %reduce-scatter.19.cloned.1.call-update) | async-done | bytes 589840 | tf_op jit(solution)/shard_map/reduce_scatter | solution.py:104
  810.4 49.9 %all-gather.21.cloned.1.call-done = bf16[2048,1152]{1,0:T(8,128)(2,1)} async-done(((bf16[256,1152]{1,0:T(8,128)(2,1)}), bf16[2048,1152]{1,0:T(8,128)(2,1)}) %all-gather.21.cloned.1.call-update) | async-done | bytes 4718608 | tf_op jit(solution)/shard_map/all_gather | solution.py:100
  860.3 9.9 fusion.179
  871.6 5.8 convolution_convert_fusion.2
  877.5 53.9 %reduce-scatter.21.cloned.1.call-done = bf16[256,1152]{1,0:T(8,128)(2,1)} async-done(((bf16[2048,1152]{1,0:T(8,128)(2,1)}), bf16[256,1152]{1,0:T(8,128)(2,1)}) %reduce-scatter.21.cloned.1.call-update) | async-done | bytes 589840 | tf_op jit(solution)/shard_map/reduce_scatter | solution.py:104
  937.0 49.7 %all-gather.23.cloned.1.call-done = bf16[2048,1152]{1,0:T(8,128)(2,1)} async-done(((bf16[256,1152]{1,0:T(8,128)(2,1)}), bf16[2048,1152]{1,0:T(8,128)(2,1)}) %all-gather.23.cloned.1.call-update) | async-done | bytes 4718608 | tf_op jit(solution)/shard_map/all_gather | solution.py:100
  986.8 4.1 convolution_convert_fusion.16
  999.2 4.6 convolution_convert_fusion
  1005.0 7.3 fusion.22
  1012.4 9.2 fusion.20
  1026.6 3.5 fusion.24
  1030.2 5.9 convolution_convert_fusion.12
  1038.2 6.4 fusion.21
  1046.4 8.2 fusion.19
  1056.7 3.5 fusion.23
  1061.1 4.9 convolution_convert_fusion.13
  1074.2 26.9 %all-reduce = (bf16[2,6912]{1,0:T(2,128)(2,1)S(1)}, bf16[2,1152]{1,0:T(2,128)(2,1)S(1)}, bf16[2,1152]{1,0:T(2,128)(2,1)S(1)}) all-reduce(bf16[2,6912]{1,0:T(2,128)(2,1)S(1)} %pad_maximum_fusion.4, bf16[2,1152]{1,0:T(2,128)(2,1)S(1)} %get-tuple-element.108, ...), channel_id=1, replica_groups=mesh['dp'=4,'tensor'=8] {'tensor'}, use_global_device_ids=true, to_apply=%region_43.44 | all-reduce | flops 18432 | bytes 73728 | tf_op jit(solution)/shard_map/psum | solution.py:298
  1108.5 18.3 %all-reduce.1 = (bf16[2,6912]{1,0:T(2,128)(2,1)S(1)}, bf16[2,2,144]{2,1,0:T(2,128)(2,1)S(1)}, bf16[2,1152]{1,0:T(2,128)(2,1)S(1)}, bf16[2,576]{1,0:T(2,128)(2,1)S(1)}, bf16[2,1152]{1,0:T(2,128)(2,1)S(1)}) all-reduce(bf16[2,6912]{1,0:T(2,128)(2,1)S(1)} %get-tuple-element.41, ...), channel_id=1, replica_groups=mesh['dp'=4,'tensor'=8] {'dp'}, use_global_device_ids=true, to_apply=%region_45.46 | all-reduce | flops 20160 | bytes 80640 | tf_op jit(solution)/shard_map/psum | solution.py:311
  1129.9 206.3 %all-reduce.5.cloned.1.call-done = (bf16[2,144,6912]{2,1,0:T(8,128)(2,1)}, bf16[2,1152,3,144]{1,3,2,0:T(8,128)(2,1)}, bf16[2,144,1152]{2,1,0:T(8,128)(2,1)}, bf1...) async-done(((bf16[2,144,6912]{2,1,0:T(8,128)(2,1)}, bf16[2,1152,3,144]{1,3,2,0:T(8,128)(2,1)}, bf16[2,144,1152]{2,1,0:T(8,128)(2,1)}, bf16[2,1152,576]{1,2,0:T(8,128)(2,1)}, ...) | async-done | bytes 11943952 | tf_op jit(solution)/shard_map/psum | solution.py:310
  1338.4 6.0 convert_element_type.427
  (439 shorter events, 140.0 us)
Async XLA Ops:
  7.2 89.7 %all-gather.9.cloned.1.call-start = ((), (), s32[]{:S(2)}) async-start(), calls=%async_computation.8 | async-start | bytes 5308416 | tf_op jit(solution)/shard_map/all_gather | solution.py:90
  9.1 36.5 %copy-start.66 = (f32[256]{0:T(256)}, f32[256]{0:T(256)S(1)}, u32[]{:S(2)}) copy-start(f32[256]{0:T(256)S(1)} %broadcast_multiply_fusion.3) | copy-start | bytes 3076
  10.5 35.1 %copy-start.78 = (f32[256]{0:T(256)}, f32[256]{0:T(256)S(1)}, u32[]{:S(2)}) copy-start(f32[256]{0:T(256)S(1)} %fusion.137) | copy-start | bytes 3076
  11.1 33.7 %copy-start.68 = (bf16[2,6912]{1,0:T(2,128)(2,1)S(1)}, bf16[2,6912]{1,0:T(2,128)(2,1)}, u32[]{:S(2)}) copy-start(bf16[2,6912]{1,0:T(2,128)(2,1)} %param.16) | copy-start | bytes 82948
  11.1 34.5 %copy-start = (bf16[1,256,1152]{2,1,0:T(8,128)(2,1)S(1)}, bf16[1,256,1152]{2,1,0:T(8,128)(2,1)}, u32[]{:S(2)}) copy-start(bf16[1,256,1152]{2,1,0:T(8,128)(2,1)} %param.13) | copy-start | bytes 1769476
  13.9 32.9 %copy-start.107 = (bf16[2,2,144]{2,1,0:T(2,128)(2,1)S(1)}, bf16[2,2,144]{2,1,0:T(2,128)(2,1)}, u32[]{:S(2)}) copy-start(bf16[2,2,144]{2,1,0:T(2,128)(2,1)} %param.18) | copy-start | bytes 3460
  13.9 32.9 %copy-start.30 = (bf16[2,1152,3,144]{1,3,2,0:T(8,128)(2,1)S(1)}, bf16[2,1152,3,144]{1,3,2,0:T(8,128)(2,1)}, u32[]{:S(2)}) copy-start(bf16[2,1152,3,144]{1,3,2,0:T(8,128)(2,1)} %param.17) | copy-start | bytes 5971972
  45.6 125.8 %copy-start.54 = (f32[1152]{0:T(1024)}, f32[1152]{0:T(1024)S(1)}, u32[]{:S(2)}) copy-start(f32[1152]{0:T(1024)S(1)} %get-tuple-element.30) | copy-start | bytes 13828
  45.6 245.9 %copy-start.59 = (f32[1152]{0:T(1024)}, f32[1152]{0:T(1024)S(1)}, u32[]{:S(2)}) copy-start(f32[1152]{0:T(1024)S(1)} %get-tuple-element.31) | copy-start | bytes 13828
  45.6 247.8 %copy-start.48 = (f32[1152]{0:T(1024)}, f32[1152]{0:T(1024)S(1)}, u32[]{:S(2)}) copy-start(f32[1152]{0:T(1024)S(1)} %get-tuple-element.27) | copy-start | bytes 13828
  46.8 121.7 %reduce-scatter.9.cloned.1.call-start = ((), (), s32[]{:S(2)}) async-start(), calls=%async_computation.9 | async-start | bytes 5308416 | tf_op jit(solution)/shard_map/reduce_scatter | solution.py:94
  114.6 108.4 %all-gather.11.cloned.1.call-start = ((), (), s32[]{:S(2)}) async-start(), calls=%async_computation.10 | async-start | bytes 5308416 | tf_op jit(solution)/shard_map/all_gather | solution.py:90
  169.9 58.7 %copy-start.69 = (f32[256]{0:T(256)}, f32[256]{0:T(256)S(1)}, u32[]{:S(2)}) copy-start(f32[256]{0:T(256)S(1)} %broadcast_multiply_fusion.2) | copy-start | bytes 3076
  171.4 57.2 %copy-start.101 = (f32[256]{0:T(256)}, f32[256]{0:T(256)S(1)}, u32[]{:S(2)}) copy-start(f32[256]{0:T(256)S(1)} %multiply_reduce_fusion.9) | copy-start | bytes 3076
  171.4 57.2 %copy-start.80 = (f32[256]{0:T(256)}, f32[256]{0:T(256)S(1)}, u32[]{:S(2)}) copy-start(f32[256]{0:T(256)S(1)} %fusion.138) | copy-start | bytes 3076
  172.7 118.8 %reduce-scatter.11.cloned.1.call-start = ((), (), s32[]{:S(2)}) async-start(), calls=%async_computation.11 | async-start | bytes 5308416 | tf_op jit(solution)/shard_map/reduce_scatter | solution.py:94
  173.6 55.0 %copy-start.109 = (f32[576]{0:T(1024)}, f32[576]{0:T(1024)S(1)}, u32[]{:S(2)}) copy-start(f32[576]{0:T(1024)S(1)} %get-tuple-element.40) | copy-start | bytes 6916
  237.6 107.1 %all-gather.13.cloned.1.call-start = ((), (), s32[]{:S(2)}) async-start(), calls=%async_computation.12 | async-start | bytes 5308416 | tf_op jit(solution)/shard_map/all_gather | solution.py:90
  238.9 55.6 %copy-start.57 = (f32[1152]{0:T(1024)}, f32[1152]{0:T(1024)S(1)}, u32[]{:S(2)}) copy-start(f32[1152]{0:T(1024)S(1)} %get-tuple-element.36) | copy-start | bytes 13828
  293.0 51.7 %copy-start.37 = (bf16[1,1152,3,144]{1,3,2,0:T(8,128)(2,1)S(1)}, bf16[1,1152,3,144]{1,3,2,0:T(8,128)(2,1)}, u32[]{:S(2)}) copy-start(bf16[1,1152,3,144]{1,3,2,0:T(8,128)(2,1)} %get-tuple-element.78) | copy-start | bytes 2985988
  293.1 56.5 %copy-start.64 = (f32[256]{0:T(256)}, f32[256]{0:T(256)S(1)}, u32[]{:S(2)}) copy-start(f32[256]{0:T(256)S(1)} %broadcast_multiply_fusion.1) | copy-start | bytes 3076
  293.3 56.2 %copy-start.103 = (f32[256]{0:T(256)}, f32[256]{0:T(256)S(1)}, u32[]{:S(2)}) copy-start(f32[256]{0:T(256)S(1)} %multiply_reduce_fusion.8) | copy-start | bytes 3076
  293.4 56.2 %copy-start.76 = (f32[256]{0:T(256)}, f32[256]{0:T(256)S(1)}, u32[]{:S(2)}) copy-start(f32[256]{0:T(256)S(1)} %fusion.139) | copy-start | bytes 3076
  294.5 132.8 %reduce-scatter.13.cloned.1.call-start = ((), (), s32[]{:S(2)}) async-start(), calls=%async_computation.13 | async-start | bytes 5308416 | tf_op jit(solution)/shard_map/reduce_scatter | solution.py:94
  373.4 108.7 %all-gather.15.cloned.1.call-start = ((), (), s32[]{:S(2)}) async-start(), calls=%async_computation.14 | async-start | bytes 5308416 | tf_op jit(solution)/shard_map/all_gather | solution.py:90
  431.9 103.0 %all-gather.17.cloned.1.call-start = ((), (), s32[]{:S(2)}) async-start(), calls=%async_computation.16 | async-start | bytes 5308416 | tf_op jit(solution)/shard_map/all_gather | solution.py:100
  434.5 171.4 %reduce-scatter.17.cloned.1.call-start = ((), (), s32[]{:S(2)}) async-start(), calls=%async_computation.17 | async-start | bytes 5308416 | tf_op jit(solution)/shard_map/reduce_scatter | solution.py:104
  552.0 110.0 %reduce-scatter.15.cloned.1.call-start = ((), (), s32[]{:S(2)}) async-start(), calls=%async_computation.15 | async-start | bytes 5308416 | tf_op jit(solution)/shard_map/reduce_scatter | solution.py:94
  562.3 155.4 %all-gather.19.cloned.1.call-start = ((), (), s32[]{:S(2)}) async-start(), calls=%async_computation.18 | async-start | bytes 5308416 | tf_op jit(solution)/shard_map/all_gather | solution.py:100
  664.7 53.0 %copy-start.41 = (bf16[2,144,1152]{2,1,0:T(8,128)(2,1)S(1)}, bf16[2,144,1152]{2,1,0:T(8,128)(2,1)}, u32[]{:S(2)}) copy-start(bf16[2,144,1152]{2,1,0:T(8,128)(2,1)} %param.19) | copy-start | bytes 1990660
  664.7 53.0 %copy-start.82 = (f32[256]{0:T(256)}, f32[256]{0:T(256)S(1)}, u32[]{:S(2)}) copy-start(f32[256]{0:T(256)S(1)} %negate_multiply_fusion.3) | copy-start | bytes 3076
  667.5 135.6 %reduce-scatter.19.cloned.1.call-start = ((), (), s32[]{:S(2)}) async-start(), calls=%async_computation.19 | async-start | bytes 5308416 | tf_op jit(solution)/shard_map/reduce_scatter | solution.py:104
  749.2 58.3 %copy-start.3 = (f32[256,1152]{1,0:T(8,128)S(1)}, f32[256,1152]{1,0:T(8,128)}, u32[]{:S(2)}) copy-start(f32[256,1152]{1,0:T(8,128)} %copy-done.2) | copy-start | bytes 3538948
  749.2 111.1 %all-gather.21.cloned.1.call-start = ((), (), s32[]{:S(2)}) async-start(), calls=%async_computation.20 | async-start | bytes 5308416 | tf_op jit(solution)/shard_map/all_gather | solution.py:100
  810.1 121.3 %reduce-scatter.21.cloned.1.call-start = ((), (), s32[]{:S(2)}) async-start(), calls=%async_computation.21 | async-start | bytes 5308416 | tf_op jit(solution)/shard_map/reduce_scatter | solution.py:104
  877.4 54.0 %copy-start.55 = (f32[1152]{0:T(1024)S(1)}, f32[1152]{0:T(1024)}, u32[]{:S(2)}) copy-start(f32[1152]{0:T(1024)} %copy-done.54) | copy-start | bytes 13828
  877.4 54.0 %copy-start.70 = (f32[256]{0:T(256)S(1)}, f32[256]{0:T(256)}, u32[]{:S(2)}) copy-start(f32[256]{0:T(256)} %copy-done.69) | copy-start | bytes 3076
  877.4 54.0 %copy-start.81 = (f32[256]{0:T(256)S(1)}, f32[256]{0:T(256)}, u32[]{:S(2)}) copy-start(f32[256]{0:T(256)} %copy-done.80) | copy-start | bytes 3076
  877.4 56.3 %copy-start.102 = (f32[256]{0:T(256)S(1)}, f32[256]{0:T(256)}, u32[]{:S(2)}) copy-start(f32[256]{0:T(256)} %copy-done.101) | copy-start | bytes 3076
  877.5 56.9 %copy-start.7 = (f32[256,1152]{1,0:T(8,128)S(1)}, f32[256,1152]{1,0:T(8,128)}, u32[]{:S(2)}) copy-start(f32[256,1152]{1,0:T(8,128)} %get-tuple-element.58) | copy-start | bytes 3538948
  877.5 109.3 %all-gather.23.cloned.1.call-start = ((), (), s32[]{:S(2)}) async-start(), calls=%async_computation.22 | async-start | bytes 5308416 | tf_op jit(solution)/shard_map/all_gather | solution.py:100
  934.4 52.4 %copy-start.42 = (bf16[2,144,1152]{2,1,0:T(8,128)(2,1)S(1)}, bf16[2,144,1152]{2,1,0:T(8,128)(2,1)}, u32[]{:S(2)}) copy-start(bf16[2,144,1152]{2,1,0:T(8,128)(2,1)} %param.19) | copy-start | bytes 1990660
  936.5 54.5 %copy-start.63 = (f32[8,2,256]{2,1,0:T(2,128)S(1)}, f32[8,2,256]{2,1,0:T(2,128)}, u32[]{:S(2)}) copy-start(f32[8,2,256]{2,1,0:T(2,128)} %copy-done.62) | copy-start | bytes 49156
  936.5 130.9 %reduce-scatter.23.cloned.1.call-start = ((), (), s32[]{:S(2)}) async-start(), calls=%async_computation.23 | async-start | bytes 5308416 | tf_op jit(solution)/shard_map/reduce_scatter | solution.py:104
  1003.8 332.4 %all-reduce.5.cloned.1.call-start = ((), (), s32[]{:S(2)}) async-start(), calls=%async_computation.24 | async-start | bytes 23887872 | tf_op jit(solution)/shard_map/psum | solution.py:310
  1012.4 11.6 copy-start.4
  1012.4 11.6 copy-start.56
  1070.9 30.2 %copy-start.108 = (f32[144]{0:T(256)S(1)}, f32[144]{0:T(256)}, u32[]{:S(2)}) copy-start(f32[144]{0:T(256)} %get-tuple-element.54) | copy-start | bytes 1732
  (93 other events, 324.9 us)
Sparse Core Ops, SparseCore 0:
  46.9 49.9 all-gather.8
  114.7 53.7 reduce-scatter.8
  172.9 50.0 all-gather.10
  237.7 53.7 reduce-scatter.10
  294.6 50.0 all-gather.12
  373.5 53.7 reduce-scatter.12
  432.0 50.0 all-gather.14
  484.3 50.5 all-gather.16
  552.1 53.7 reduce-scatter.16
  608.7 53.3 reduce-scatter.14
  667.6 50.0 all-gather.18
  749.3 53.7 reduce-scatter.18
  810.2 50.0 all-gather.20
  877.6 53.7 reduce-scatter.20
  936.6 50.0 all-gather.22
  1003.9 53.7 reduce-scatter.22
  1103.7 232.4 all-reduce.4
where the time goes:
time: 1370 us; the launch traced here: 1360 us
  waiting for transfers between devices  959 us (70%)
  matrix products  176 us (13%)
  other arithmetic  82.1 us (6%)
  blocking collectives  76 us (6%)
  local copies, waits for them, and re-layouts  48.3 us (4%)
  between operations  16 us (1%)
    reduce_scatter x4, waiting for transfers between devices, reduce_rows(): lax.psum_scatter(partial_terms.astype(jnp.bfloat16), 'tensor', scatter_di...  212 us
    psum x1, waiting for transfers between devices, per_device(): lax.psum(ada_w_grad.astype(jnp.bfloat16), 'dp').astype(jnp.float32)  206 us
    all_gather x4, waiting for transfers between devices, spread_rows(): return lax.all_gather(row_block, 'tensor', axis=0, tiled=True)  195 us
    all_gather x4, waiting for transfers between devices, spread_grads(): return lax.all_gather(row_block, 'tensor', axis=0, tiled=True)  194 us
    reduce_scatter x4, waiting for transfers between devices, reduce_grads(): lax.psum_scatter(partial_terms.astype(jnp.bfloat16), 'tensor', scatter_di...  151 us
    psum x1, blocking collectives, per_device(): modulations = lax.psum(ada_terms, 'tensor') + ada_bias.astype(jnp.float32)  30.9 us
    unnamed x278, local copies, waits for them, and re-layouts  27.9 us
  transfers between devices with their start and end apart: 17, of which 16 were waited for; matrix products, arithmetic and copies ran while one was open for 7% of the time, Pallas kernels for 0%

commit v1 on v0

--- a/solution.py
+++ b/solution.py
@@ -8,6 +8,11 @@
 PATCHES = 256
 FRAMES = 8
 LAYERS = 2
+
+
+def add_all(x, axis):
+    blocks = lax.all_gather(x, axis)
+    return jnp.sum(blocks, axis=0)
 
 
 def normalize(stream):
@@ -307,7 +312,7 @@
     silu_grad = jnp.einsum("lm,ldm->d", mod_low, ada_weight, preferred_element_type=jnp.float32)
     cond_grad = silu_back(silu_grad)[0]
     summed = (
-        lax.psum(ada_w_grad.astype(jnp.bfloat16), "dp").astype(jnp.float32),
+        add_all(ada_w_grad.astype(jnp.bfloat16), "dp").astype(jnp.float32),
         lax.psum(ada_b_grad.astype(jnp.bfloat16), "dp").astype(jnp.float32),
         lax.psum(collect(0).astype(jnp.bfloat16), "dp").astype(jnp.float32),
         lax.psum(collect(1).astype(jnp.bfloat16), "dp").astype(jnp.float32),

time: 1370 us -> 1410 us (1.029)
  waiting for transfers between devices: 959 us -> 1000 us
  matrix products: 176 us -> 156 us
  other arithmetic: 82.1 us -> 96.7 us
    all_gather x0 -> x1, waiting for transfers between devices: none -> 119 us  [add_all(): blocks = lax.all_gather(x, axis)]
    psum x1, waiting for transfers between devices: 206 us -> 128 us  [per_device(): lax.psum(collect(0).astype(jnp.bfloat16), 'dp').astype(jnp.float32)]
    unnamed x278 -> x274, local copies, waits for them, and re-layouts: 27.9 us -> 33.1 us
  transfers between devices with their start and end apart: 17 -> 18, of which waited for: 16 -> 17; matrix products, arithmetic and copies ran while one was open for 7% -> 8% of each run, Pallas kernels for 0% -> 0%
where the time goes in v1:
time: 1410 us; the launch traced here: 1400 us
  waiting for transfers between devices  1000 us (71%)
  matrix products  156 us (11%)
  other arithmetic  96.7 us (7%)
  blocking collectives  75.8 us (5%)
  local copies, waits for them, and re-layouts  57.3 us (4%)
  between operations  16.3 us (1%)
    reduce_scatter x4, waiting for transfers between devices, reduce_rows(): lax.psum_scatter(partial_terms.astype(jnp.bfloat16), 'tensor', scatter_di...  212 us
    all_gather x4, waiting for transfers between devices, spread_rows(): return lax.all_gather(row_block, 'tensor', axis=0, tiled=True)  195 us
    all_gather x4, waiting for transfers between devices, spread_grads(): return lax.all_gather(row_block, 'tensor', axis=0, tiled=True)  194 us
    reduce_scatter x4, waiting for transfers between devices, reduce_grads(): lax.psum_scatter(partial_terms.astype(jnp.bfloat16), 'tensor', scatter_di...  151 us
    psum x1, waiting for transfers between devices, per_device(): lax.psum(collect(0).astype(jnp.bfloat16), 'dp').astype(jnp.float32)  128 us
    all_gather x1, waiting for transfers between devices, add_all(): blocks = lax.all_gather(x, axis)  119 us
    unnamed x274, local copies, waits for them, and re-layouts  33.1 us
    psum x1, blocking collectives, per_device(): modulations = lax.psum(ada_terms, 'tensor') + ada_bias.astype(jnp.float32)  30.9 us
  transfers between devices with their start and end apart: 18, of which 17 were waited for; matrix products, arithmetic and copies ran while one was open for 8% of the time, Pallas kernels for 0%

profile of v1, /device:TPU:0, one launch (start us, length us, event | category | flops | bytes accessed | tf_op | source)
XLA Modules:
  0.0 1404.6 jit_solution(7734177035820186794)
XLA Ops:
  14.0 30.9 %psum.91 = f32[2,6912]{1,0:T(2,128)S(1)} all-reduce(f32[2,6912]{1,0:T(2,128)S(1)} %bitcast.364), channel_id=1, replica_groups=mesh['dp'=4,'tensor'=8] {'tensor'}, use_global_device_ids=true, to_apply=%region_0.1 | all-reduce | flops 13824 | bytes 110592 | tf_op jit(solution)/shard_map/psum | solution.py:268
  48.3 48.5 %all-gather.10.cloned.1.call-done = bf16[2048,1152]{1,0:T(8,128)(2,1)} async-done(((bf16[256,1152]{1,0:T(8,128)(2,1)}), bf16[2048,1152]{1,0:T(8,128)(2,1)}) %all-gather.10.cloned.1.call-update) | async-done | bytes 4718608 | tf_op jit(solution)/shard_map/all_gather | solution.py:95
  96.8 5.1 fusion.181
  104.4 3.2 fusion.168
  110.8 3.8 convolution_convert_fusion.7
  115.8 52.6 %reduce-scatter.9.cloned.1.call-done = bf16[256,1152]{1,0:T(8,128)(2,1)} async-done(((bf16[2048,1152]{1,0:T(8,128)(2,1)}), bf16[256,1152]{1,0:T(8,128)(2,1)}) %reduce-scatter.9.cloned.1.call-update) | async-done | bytes 589840 | tf_op jit(solution)/shard_map/reduce_scatter | solution.py:99
  173.6 49.3 %all-gather.12.cloned.1.call-done = bf16[2048,1152]{1,0:T(8,128)(2,1)} async-done(((bf16[256,1152]{1,0:T(8,128)(2,1)}), bf16[2048,1152]{1,0:T(8,128)(2,1)}) %all-gather.12.cloned.1.call-update) | async-done | bytes 4718608 | tf_op jit(solution)/shard_map/all_gather | solution.py:95
  223.0 5.6 fusion.59
  230.9 6.7 convolution_convert_fusion.6
  238.9 52.6 %reduce-scatter.11.cloned.1.call-done = bf16[256,1152]{1,0:T(8,128)(2,1)} async-done(((bf16[2048,1152]{1,0:T(8,128)(2,1)}), bf16[256,1152]{1,0:T(8,128)(2,1)}) %reduce-scatter.11.cloned.1.call-update) | async-done | bytes 589840 | tf_op jit(solution)/shard_map/reduce_scatter | solution.py:99
  294.6 50.2 %all-gather.14.cloned.1.call-done = bf16[2048,1152]{1,0:T(8,128)(2,1)} async-done(((bf16[256,1152]{1,0:T(8,128)(2,1)}), bf16[2048,1152]{1,0:T(8,128)(2,1)}) %all-gather.14.cloned.1.call-update) | async-done | bytes 4718608 | tf_op jit(solution)/shard_map/all_gather | solution.py:95
  344.7 4.8 fusion.182
  356.7 5.3 fusion.169
  362.0 3.7 fusion.40
  368.6 4.8 convolution_convert_fusion.5
  373.5 53.9 %reduce-scatter.13.cloned.1.call-done = bf16[256,1152]{1,0:T(8,128)(2,1)} async-done(((bf16[2048,1152]{1,0:T(8,128)(2,1)}), bf16[256,1152]{1,0:T(8,128)(2,1)}) %reduce-scatter.13.cloned.1.call-update) | async-done | bytes 589840 | tf_op jit(solution)/shard_map/reduce_scatter | solution.py:99
  435.0 47.1 %all-gather.16.cloned.1.call-done = bf16[2048,1152]{1,0:T(8,128)(2,1)} async-done(((bf16[256,1152]{1,0:T(8,128)(2,1)}), bf16[2048,1152]{1,0:T(8,128)(2,1)}) %all-gather.16.cloned.1.call-update) | async-done | bytes 4718608 | tf_op jit(solution)/shard_map/all_gather | solution.py:95
  482.1 8.2 fusion.51
  490.3 44.6 %all-gather.18.cloned.1.call-done = bf16[2048,1152]{1,0:T(8,128)(2,1)} async-done(((bf16[256,1152]{1,0:T(8,128)(2,1)}), bf16[2048,1152]{1,0:T(8,128)(2,1)}) %all-gather.18.cloned.1.call-update) | async-done | bytes 4718608 | tf_op jit(solution)/shard_map/all_gather | solution.py:105
  534.9 9.9 fusion.178
  546.2 5.8 convolution_convert_fusion.3
  552.3 10.0 convolution_convert_fusion.4
  562.4 43.6 %reduce-scatter.17.cloned.1.call-done = bf16[256,1152]{1,0:T(8,128)(2,1)} async-done(((bf16[2048,1152]{1,0:T(8,128)(2,1)}), bf16[256,1152]{1,0:T(8,128)(2,1)}) %reduce-scatter.17.cloned.1.call-update) | async-done | bytes 589840 | tf_op jit(solution)/shard_map/reduce_scatter | solution.py:109
  609.3 52.7 %reduce-scatter.15.cloned.1.call-done = bf16[256,1152]{1,0:T(8,128)(2,1)} async-done(((bf16[2048,1152]{1,0:T(8,128)(2,1)}), bf16[256,1152]{1,0:T(8,128)(2,1)}) %reduce-scatter.15.cloned.1.call-update) | async-done | bytes 589840 | tf_op jit(solution)/shard_map/reduce_scatter | solution.py:99
  667.8 49.9 %all-gather.20.cloned.1.call-done = bf16[2048,1152]{1,0:T(8,128)(2,1)} async-done(((bf16[256,1152]{1,0:T(8,128)(2,1)}), bf16[2048,1152]{1,0:T(8,128)(2,1)}) %all-gather.20.cloned.1.call-update) | async-done | bytes 4718608 | tf_op jit(solution)/shard_map/all_gather | solution.py:105
  717.7 4.0 convolution_convert_fusion.17
  723.7 4.2 fusion.174
  744.5 4.6 convolution_convert_fusion.1
  749.2 53.9 %reduce-scatter.19.cloned.1.call-done = bf16[256,1152]{1,0:T(8,128)(2,1)} async-done(((bf16[2048,1152]{1,0:T(8,128)(2,1)}), bf16[256,1152]{1,0:T(8,128)(2,1)}) %reduce-scatter.19.cloned.1.call-update) | async-done | bytes 589840 | tf_op jit(solution)/shard_map/reduce_scatter | solution.py:109
  810.6 49.7 %all-gather.22.cloned.1.call-done = bf16[2048,1152]{1,0:T(8,128)(2,1)} async-done(((bf16[256,1152]{1,0:T(8,128)(2,1)}), bf16[2048,1152]{1,0:T(8,128)(2,1)}) %all-gather.22.cloned.1.call-update) | async-done | bytes 4718608 | tf_op jit(solution)/shard_map/all_gather | solution.py:105
  860.3 9.9 fusion.179
  870.1 5.8 convolution_convert_fusion.2
  876.1 53.9 %reduce-scatter.21.cloned.1.call-done = bf16[256,1152]{1,0:T(8,128)(2,1)} async-done(((bf16[2048,1152]{1,0:T(8,128)(2,1)}), bf16[256,1152]{1,0:T(8,128)(2,1)}) %reduce-scatter.21.cloned.1.call-update) | async-done | bytes 589840 | tf_op jit(solution)/shard_map/reduce_scatter | solution.py:109
  935.1 50.2 %all-gather.24.cloned.1.call-done = bf16[2048,1152]{1,0:T(8,128)(2,1)} async-done(((bf16[256,1152]{1,0:T(8,128)(2,1)}), bf16[2048,1152]{1,0:T(8,128)(2,1)}) %all-gather.24.cloned.1.call-update) | async-done | bytes 4718608 | tf_op jit(solution)/shard_map/all_gather | solution.py:105
  985.3 4.1 convolution_convert_fusion.16
  997.7 4.6 convolution_convert_fusion
  1002.5 6.4 fusion.22
  1009.0 8.1 fusion.20
  1017.1 3.5 fusion.24
  1023.2 3.2 fusion.21
  1028.3 4.5 fusion.19
  1066.8 27.6 %all-reduce = (bf16[2,6912]{1,0:T(2,128)(2,1)S(1)}, bf16[2,1152]{1,0:T(2,128)(2,1)S(1)}, bf16[2,1152]{1,0:T(2,128)(2,1)S(1)}) all-reduce(bf16[2,6912]{1,0:T(2,128)(2,1)S(1)} %pad_maximum_fusion.4, bf16[2,1152]{1,0:T(2,128)(2,1)S(1)} %get-tuple-element.107, ...), channel_id=1, replica_groups=mesh['dp'=4,'tensor'=8] {'tensor'}, use_global_device_ids=true, to_apply=%region_43.44 | all-reduce | flops 18432 | bytes 73728 | tf_op jit(solution)/shard_map/psum | solution.py:303
  1098.0 128.0 %all-reduce.5.cloned.1.call-done = (bf16[2,1152,3,144]{1,3,2,0:T(8,128)(2,1)}, bf16[2,144,1152]{2,1,0:T(8,128)(2,1)}, bf16[2,1152,576]{1,2,0:T(8,128)(2,1)}, bf16[2,576,1152]{2,1,0:T(8,128)(2,1)}) async-done(((bf16[2,1152,3,144]{1,3,2,0:T(8,128)(2,1)}, bf16[2,144,1152]{2,1,0:T(8,128)(2,1)}, bf16[2,1152,576]{1,2,0:T(8,128)(2,1)}, bf16[2,576,1152]{2,1,0:T(8,128)(2,1)}), (bf16[2,1152,3,144]{1,3,2,0:T(8,128)(2,1)}, ...) | async-done | bytes 7962640 | tf_op jit(solution)/shard_map/psum | solution.py:317
  1234.2 3.4 convert_element_type.452
  1240.7 17.3 %all-reduce.1 = (bf16[2,6912]{1,0:T(2,128)(2,1)S(1)}, bf16[2,2,144]{2,1,0:T(2,128)(2,1)S(1)}, bf16[2,1152]{1,0:T(2,128)(2,1)S(1)}, bf16[2,576]{1,0:T(2,128)(2,1)S(1)}, bf16[2,1152]{1,0:T(2,128)(2,1)S(1)}) all-reduce(bf16[2,6912]{1,0:T(2,128)(2,1)S(1)} %get-tuple-element.41, ...), channel_id=1, replica_groups=mesh['dp'=4,'tensor'=8] {'dp'}, use_global_device_ids=true, to_apply=%region_45.46 | all-reduce | flops 20160 | bytes 80640 | tf_op jit(solution)/shard_map/psum | solution.py:316
  1261.0 118.9 %all-gather.26.cloned.1.call-done = bf16[4,2,144,6912]{3,2,1,0:T(8,128)(2,1)} async-done(((bf16[1,2,144,6912]{3,2,1,0:T(8,128)(2,1)}), bf16[4,2,144,6912]{3,2,1,0:T(8,128)(2,1)}) %all-gather.26.cloned.1.call-update) | async-done | bytes 15925264 | tf_op jit(solution)/shard_map/all_gather | solution.py:14
  1379.9 11.5 reduce_sum.436
  1391.4 5.9 convert_element_type.436
  (445 shorter events, 152.4 us)
Async XLA Ops:
  7.2 89.7 %all-gather.10.cloned.1.call-start = ((), (), s32[]{:S(2)}) async-start(), calls=%async_computation.8 | async-start | bytes 5308416 | tf_op jit(solution)/shard_map/all_gather | solution.py:95
  9.1 36.5 %copy-start.61 = (f32[256]{0:T(256)}, f32[256]{0:T(256)S(1)}, u32[]{:S(2)}) copy-start(f32[256]{0:T(256)S(1)} %broadcast_multiply_fusion.3) | copy-start | bytes 3076
  10.5 35.1 %copy-start.73 = (f32[256]{0:T(256)}, f32[256]{0:T(256)S(1)}, u32[]{:S(2)}) copy-start(f32[256]{0:T(256)S(1)} %fusion.137) | copy-start | bytes 3076
  11.1 33.7 %copy-start.63 = (bf16[2,6912]{1,0:T(2,128)(2,1)S(1)}, bf16[2,6912]{1,0:T(2,128)(2,1)}, u32[]{:S(2)}) copy-start(bf16[2,6912]{1,0:T(2,128)(2,1)} %param.16) | copy-start | bytes 82948
  11.1 34.5 %copy-start = (bf16[1,256,1152]{2,1,0:T(8,128)(2,1)S(1)}, bf16[1,256,1152]{2,1,0:T(8,128)(2,1)}, u32[]{:S(2)}) copy-start(bf16[1,256,1152]{2,1,0:T(8,128)(2,1)} %param.13) | copy-start | bytes 1769476
  13.9 32.9 %copy-start.92 = (bf16[2,2,144]{2,1,0:T(2,128)(2,1)S(1)}, bf16[2,2,144]{2,1,0:T(2,128)(2,1)}, u32[]{:S(2)}) copy-start(bf16[2,2,144]{2,1,0:T(2,128)(2,1)} %param.18) | copy-start | bytes 3460
  13.9 32.9 %copy-start.29 = (bf16[2,1152,3,144]{1,3,2,0:T(8,128)(2,1)S(1)}, bf16[2,1152,3,144]{1,3,2,0:T(8,128)(2,1)}, u32[]{:S(2)}) copy-start(bf16[2,1152,3,144]{1,3,2,0:T(8,128)(2,1)} %param.17) | copy-start | bytes 5971972
  45.6 125.9 %copy-start.50 = (f32[1152]{0:T(1024)}, f32[1152]{0:T(1024)S(1)}, u32[]{:S(2)}) copy-start(f32[1152]{0:T(1024)S(1)} %get-tuple-element.30) | copy-start | bytes 13828
  45.6 245.9 %copy-start.54 = (f32[1152]{0:T(1024)}, f32[1152]{0:T(1024)S(1)}, u32[]{:S(2)}) copy-start(f32[1152]{0:T(1024)S(1)} %get-tuple-element.31) | copy-start | bytes 13828
  45.6 247.8 %copy-start.44 = (f32[1152]{0:T(1024)}, f32[1152]{0:T(1024)S(1)}, u32[]{:S(2)}) copy-start(f32[1152]{0:T(1024)S(1)} %get-tuple-element.27) | copy-start | bytes 13828
  46.8 121.7 %reduce-scatter.9.cloned.1.call-start = ((), (), s32[]{:S(2)}) async-start(), calls=%async_computation.9 | async-start | bytes 5308416 | tf_op jit(solution)/shard_map/reduce_scatter | solution.py:99
  114.6 108.4 %all-gather.12.cloned.1.call-start = ((), (), s32[]{:S(2)}) async-start(), calls=%async_computation.10 | async-start | bytes 5308416 | tf_op jit(solution)/shard_map/all_gather | solution.py:95
  170.0 58.7 %copy-start.64 = (f32[256]{0:T(256)}, f32[256]{0:T(256)S(1)}, u32[]{:S(2)}) copy-start(f32[256]{0:T(256)S(1)} %broadcast_multiply_fusion.2) | copy-start | bytes 3076
  171.4 57.2 %copy-start.86 = (f32[256]{0:T(256)}, f32[256]{0:T(256)S(1)}, u32[]{:S(2)}) copy-start(f32[256]{0:T(256)S(1)} %multiply_reduce_fusion.9) | copy-start | bytes 3076
  171.4 57.2 %copy-start.75 = (f32[256]{0:T(256)}, f32[256]{0:T(256)S(1)}, u32[]{:S(2)}) copy-start(f32[256]{0:T(256)S(1)} %fusion.138) | copy-start | bytes 3076
  172.7 118.8 %reduce-scatter.11.cloned.1.call-start = ((), (), s32[]{:S(2)}) async-start(), calls=%async_computation.11 | async-start | bytes 5308416 | tf_op jit(solution)/shard_map/reduce_scatter | solution.py:99
  173.6 55.0 %copy-start.94 = (f32[576]{0:T(1024)}, f32[576]{0:T(1024)S(1)}, u32[]{:S(2)}) copy-start(f32[576]{0:T(1024)S(1)} %get-tuple-element.40) | copy-start | bytes 6916
  237.6 107.1 %all-gather.14.cloned.1.call-start = ((), (), s32[]{:S(2)}) async-start(), calls=%async_computation.12 | async-start | bytes 5308416 | tf_op jit(solution)/shard_map/all_gather | solution.py:95
  238.9 55.6 %copy-start.53 = (f32[1152]{0:T(1024)}, f32[1152]{0:T(1024)S(1)}, u32[]{:S(2)}) copy-start(f32[1152]{0:T(1024)S(1)} %get-tuple-element.36) | copy-start | bytes 13828
  293.1 51.7 %copy-start.34 = (bf16[1,1152,3,144]{1,3,2,0:T(8,128)(2,1)S(1)}, bf16[1,1152,3,144]{1,3,2,0:T(8,128)(2,1)}, u32[]{:S(2)}) copy-start(bf16[1,1152,3,144]{1,3,2,0:T(8,128)(2,1)} %get-tuple-element.77) | copy-start | bytes 2985988
  293.1 56.5 %copy-start.59 = (f32[256]{0:T(256)}, f32[256]{0:T(256)S(1)}, u32[]{:S(2)}) copy-start(f32[256]{0:T(256)S(1)} %broadcast_multiply_fusion.1) | copy-start | bytes 3076
  293.4 56.2 %copy-start.88 = (f32[256]{0:T(256)}, f32[256]{0:T(256)S(1)}, u32[]{:S(2)}) copy-start(f32[256]{0:T(256)S(1)} %multiply_reduce_fusion.8) | copy-start | bytes 3076
  293.4 56.2 %copy-start.71 = (f32[256]{0:T(256)}, f32[256]{0:T(256)S(1)}, u32[]{:S(2)}) copy-start(f32[256]{0:T(256)S(1)} %fusion.139) | copy-start | bytes 3076
  294.5 132.8 %reduce-scatter.13.cloned.1.call-start = ((), (), s32[]{:S(2)}) async-start(), calls=%async_computation.13 | async-start | bytes 5308416 | tf_op jit(solution)/shard_map/reduce_scatter | solution.py:99
  373.4 108.7 %all-gather.16.cloned.1.call-start = ((), (), s32[]{:S(2)}) async-start(), calls=%async_computation.14 | async-start | bytes 5308416 | tf_op jit(solution)/shard_map/all_gather | solution.py:95
  431.9 103.0 %all-gather.18.cloned.1.call-start = ((), (), s32[]{:S(2)}) async-start(), calls=%async_computation.16 | async-start | bytes 5308416 | tf_op jit(solution)/shard_map/all_gather | solution.py:105
  434.6 171.4 %reduce-scatter.17.cloned.1.call-start = ((), (), s32[]{:S(2)}) async-start(), calls=%async_computation.17 | async-start | bytes 5308416 | tf_op jit(solution)/shard_map/reduce_scatter | solution.py:109
  552.1 110.0 %reduce-scatter.15.cloned.1.call-start = ((), (), s32[]{:S(2)}) async-start(), calls=%async_computation.15 | async-start | bytes 5308416 | tf_op jit(solution)/shard_map/reduce_scatter | solution.py:99
  562.3 155.4 %all-gather.20.cloned.1.call-start = ((), (), s32[]{:S(2)}) async-start(), calls=%async_computation.18 | async-start | bytes 5308416 | tf_op jit(solution)/shard_map/all_gather | solution.py:105
  664.8 53.0 %copy-start.37 = (bf16[2,144,1152]{2,1,0:T(8,128)(2,1)S(1)}, bf16[2,144,1152]{2,1,0:T(8,128)(2,1)}, u32[]{:S(2)}) copy-start(bf16[2,144,1152]{2,1,0:T(8,128)(2,1)} %param.19) | copy-start | bytes 1990660
  664.8 53.0 %copy-start.77 = (f32[256]{0:T(256)}, f32[256]{0:T(256)S(1)}, u32[]{:S(2)}) copy-start(f32[256]{0:T(256)S(1)} %negate_multiply_fusion.3) | copy-start | bytes 3076
  667.5 135.6 %reduce-scatter.19.cloned.1.call-start = ((), (), s32[]{:S(2)}) async-start(), calls=%async_computation.19 | async-start | bytes 5308416 | tf_op jit(solution)/shard_map/reduce_scatter | solution.py:109
  749.2 58.3 %copy-start.3 = (f32[256,1152]{1,0:T(8,128)S(1)}, f32[256,1152]{1,0:T(8,128)}, u32[]{:S(2)}) copy-start(f32[256,1152]{1,0:T(8,128)} %copy-done.2) | copy-start | bytes 3538948
  749.2 111.1 %all-gather.22.cloned.1.call-start = ((), (), s32[]{:S(2)}) async-start(), calls=%async_computation.20 | async-start | bytes 5308416 | tf_op jit(solution)/shard_map/all_gather | solution.py:105
  810.1 119.9 %reduce-scatter.21.cloned.1.call-start = ((), (), s32[]{:S(2)}) async-start(), calls=%async_computation.21 | async-start | bytes 5308416 | tf_op jit(solution)/shard_map/reduce_scatter | solution.py:109
  876.0 54.0 %copy-start.51 = (f32[1152]{0:T(1024)S(1)}, f32[1152]{0:T(1024)}, u32[]{:S(2)}) copy-start(f32[1152]{0:T(1024)} %copy-done.50) | copy-start | bytes 13828
  876.0 54.0 %copy-start.65 = (f32[256]{0:T(256)S(1)}, f32[256]{0:T(256)}, u32[]{:S(2)}) copy-start(f32[256]{0:T(256)} %copy-done.64) | copy-start | bytes 3076
  876.0 54.0 %copy-start.76 = (f32[256]{0:T(256)S(1)}, f32[256]{0:T(256)}, u32[]{:S(2)}) copy-start(f32[256]{0:T(256)} %copy-done.75) | copy-start | bytes 3076
  876.0 56.3 %copy-start.87 = (f32[256]{0:T(256)S(1)}, f32[256]{0:T(256)}, u32[]{:S(2)}) copy-start(f32[256]{0:T(256)} %copy-done.86) | copy-start | bytes 3076
  876.0 56.9 %copy-start.8 = (f32[256,1152]{1,0:T(8,128)S(1)}, f32[256,1152]{1,0:T(8,128)}, u32[]{:S(2)}) copy-start(f32[256,1152]{1,0:T(8,128)} %get-tuple-element.57) | copy-start | bytes 3538948
  876.0 109.3 %all-gather.24.cloned.1.call-start = ((), (), s32[]{:S(2)}) async-start(), calls=%async_computation.22 | async-start | bytes 5308416 | tf_op jit(solution)/shard_map/all_gather | solution.py:105
  932.9 52.3 %copy-start.38 = (bf16[2,144,1152]{2,1,0:T(8,128)(2,1)S(1)}, bf16[2,144,1152]{2,1,0:T(8,128)(2,1)}, u32[]{:S(2)}) copy-start(bf16[2,144,1152]{2,1,0:T(8,128)(2,1)} %param.19) | copy-start | bytes 1990660
  935.1 54.5 %copy-start.58 = (f32[8,2,256]{2,1,0:T(2,128)S(1)}, f32[8,2,256]{2,1,0:T(2,128)}, u32[]{:S(2)}) copy-start(f32[8,2,256]{2,1,0:T(2,128)} %copy-done.57) | copy-start | bytes 49156
  935.1 124.0 %reduce-scatter.23.cloned.1.call-start = ((), (), s32[]{:S(2)}) async-start(), calls=%async_computation.23 | async-start | bytes 5308416 | tf_op jit(solution)/shard_map/reduce_scatter | solution.py:109
  1002.3 223.6 %all-reduce.5.cloned.1.call-start = ((), (), s32[]{:S(2)}) async-start(), calls=%async_computation.25 | async-start | bytes 15925248 | tf_op jit(solution)/shard_map/psum | solution.py:317
  1002.5 18.1 %slice-start.6 = ((s8[4718592]{0:T(1024)(128)(4,1)}), s8[4194304]{0:T(1024)(128)(4,1)S(1)}, s32[]{:S(2)}) async-start(s8[4718592]{0:T(1024)(128)(4,1)} %bitcast.376), calls=%async_computation.32 | async-start | bytes 8388608
  1040.4 339.5 %all-gather.26.cloned.1.call-start = ((), (), s32[]{:S(2)}) async-start(), calls=%async_computation.24 | async-start | bytes 19906560 | tf_op jit(solution)/shard_map/all_gather | solution.py:14
  1062.7 31.7 %copy-start.93 = (f32[144]{0:T(256)S(1)}, f32[144]{0:T(256)}, u32[]{:S(2)}) copy-start(f32[144]{0:T(256)} %get-tuple-element.53) | copy-start | bytes 1732
  (92 other events, 379.3 us)
Sparse Core Ops, SparseCore 0:
  46.9 49.9 all-gather.9
  114.7 53.7 reduce-scatter.8
  172.9 50.0 all-gather.11
  237.7 53.7 reduce-scatter.10
  294.6 50.0 all-gather.13
  373.5 53.7 reduce-scatter.12
  432.0 50.0 all-gather.15
  484.3 50.5 all-gather.17
  552.2 53.7 reduce-scatter.16
  608.7 53.3 reduce-scatter.14
  667.6 50.0 all-gather.19
  749.3 53.7 reduce-scatter.18
  810.2 50.0 all-gather.21
  876.1 53.7 reduce-scatter.20
  935.2 50.0 all-gather.23
  1002.4 53.7 reduce-scatter.22
  1061.2 164.7 all-reduce.4
  1228.4 151.5 all-gather.25
